TPU v7x, 512 devices: a whole 4x8x8 slice. The times are simulated.
512 devices in a mesh: cuts: 4 (over y_hi, core), mode: 128 (over x, y_lo, z).
Axes of the slice: x: 4, y: 8 (y_hi: 2, y_lo: 4; y = y_hi * 4 + y_lo), z: 8, core: 2. Of those that a mesh axis runs over, the one named last changes fastest.
Arguments:
- stem: bfloat16 [4, 2, 1024, 16384], P('cuts', None, None, 'mode'), may hold values from -6 to 6
- branches: bfloat16 [3, 2, 1024, 1024], P(None, None, None, 'mode'), may hold values from -0.125 to 0.125
- order: int32 [3], replicated, may hold values from 0 to 2, each once
- swap_order: int32 [3, 1024], replicated, may hold values from 0 to 1023, each once within a row
- row_bits: int32 [2048], replicated, may hold values from 0 to 1023
- column_bits: int32 [2048], replicated, may hold values from 0 to 16383
Outputs:
- stem_out: bfloat16 [4, 2, 1024, 16384], P('cuts', None, None, 'mode')
- amplitudes: float32 [2, 2048], P(None, ('cuts', 'mode'))
All inputs are finite; a program needn't handle non-finite values.
Results may differ from a plain program's by a relative error of at most 0.009.
Values may be sent and summed in bfloat16 or wider, within the bound.
A program may use at most 128 MiB of HBM per device.

v0:
```python
import jax
import jax.numpy as jnp
from jax import lax
from jax.sharding import Mesh
from jax.sharding import PartitionSpec as P

MODE = ("mode_0", "mode_1", "mode_2")
CUTS_MODE = ("cuts_0", "cuts_1", "mode_0", "mode_1", "mode_2")
CUTS = ("cuts_0", "cuts_1")


def cut_rows(length, count):
    unit = 8 if length >= 8 * count else 1
    return [length // unit * k // count * unit for k in range(1, count)]


def gather_in_order(shard, axes, turns):
    blocks = shard[None]
    for k in turns:
        blocks = lax.all_gather(blocks, axes[k], axis=0, tiled=True)
    held = [lax.axis_size(axes[k]) for k in reversed(turns)]
    blocks = blocks.reshape(*held, *shard.shape)
    turned = sorted(range(len(turns)), key=lambda place: turns[len(turns) - 1 - place])
    return blocks.transpose(*turned, *range(len(turns), blocks.ndim)).reshape(-1, *shard.shape)


def joined_along(blocks, dim):
    blocks = jnp.moveaxis(blocks, 0, dim)
    dims = blocks.shape
    return blocks.reshape(*dims[:dim], dims[dim] * dims[dim + 1], *dims[dim + 2 :])


def gather_at_once(shard, axes, dim):
    cut = max(range(max(1, shard.ndim - 1)), key=lambda d: shard.shape[d])
    count, finished = (len(axes), [])
    for initial, slab in enumerate(jnp.split(shard, cut_rows(shard.shape[cut], count), axis=cut)):
        if slab.size:
            turns = [(initial - k) % count for k in range(count)]
            finished.append(gather_in_order(slab, axes, turns))
    return joined_along(jnp.concatenate(finished, axis=cut + 1), dim)


def over_axes(shard, axes):
    for axis in axes:
        shard = lax.psum(shard, axis)
    return shard


def absorb(matrix, part):
    numbers = (((0,), (0,)), ((), ()))

    def product(left, right):
        return lax.dot_general(left, right, numbers, preferred_element_type=jnp.float32)

    real = product(matrix[0], part[0]) - product(matrix[1], part[1])
    imag = product(matrix[0], part[1]) + product(matrix[1], part[0])
    return jnp.stack([real, imag], axis=0)


def body(stem, branches, order, swap_order, row_bits, column_bits):
    local = stem[0]
    groups = lax.axis_size(MODE)
    width = local.shape[1]
    rows = local.shape[2]
    everything = gather_at_once(branches, MODE, 3)
    for step in range(swap_order.shape[0]):
        moved = jnp.take(local, swap_order[step], axis=1)
        view = moved.reshape(2, groups, width // groups, rows)
        swapped = lax.all_to_all(view, MODE, split_axis=1, concat_axis=1, tiled=True)
        current = swapped.reshape(2, width, rows)
        pick = order[step]
        matrix = lax.dynamic_index_in_dim(everything, pick, 0, keepdims=False)
        local = absorb(matrix, current).astype(jnp.bfloat16)
    offset = lax.axis_index(MODE) * rows
    column_local = column_bits - offset
    inside = jnp.logical_and(column_local >= 0, column_local < rows)
    flat_index = row_bits * rows + jnp.clip(column_local, 0, rows - 1)
    flat = local.reshape(2, width * rows)
    values = jnp.take(flat, flat_index, axis=1).astype(jnp.float32)
    values = jnp.where(inside[None, :], values, jnp.zeros_like(values))
    total_amps = over_axes(values, CUTS_MODE)
    share = values.shape[1] // lax.axis_size(CUTS_MODE)
    amplitudes = lax.dynamic_slice_in_dim(total_amps, lax.axis_index(CUTS_MODE) * share, share, 1)
    return (local[None], amplitudes)


def solution(mesh):
    finer = Mesh(
        mesh.devices.reshape(2, 2, 4, 4, 8), ("cuts_0", "cuts_1", "mode_0", "mode_1", "mode_2")
    )
    placed = (P(CUTS, None, None, MODE), P(None, None, None, MODE), P(), P(), P(), P())
    return jax.shard_map(
        body,
        mesh=finer,
        in_specs=placed,
        out_specs=(P(CUTS, None, None, MODE), P(None, CUTS_MODE)),
        check_vma=False,
    )
```

profile of v0, /device:TPU:4, one launch (start us, length us, event | category | flops | bytes accessed | tf_op | source)
XLA Modules:
  0.0 671.8 jit_solution(10324625984427429543)
XLA Ops:
  7.2 0.9 fusion.45
  8.1 33.4 %all-gather.2 = bf16[24,2,344,8]{2,3,1,0:T(8,128)(2,1)} all-gather(bf16[3,2,344,8]{2,3,1,0:T(8,128)(2,1)S(1)} %get-tuple-element.14), channel_id=4, replica_groups=mesh['cuts_0'=2,'cuts_1'=2,'mode_0'=4,'mode_1'=4,'mode_2'=8] {'mode_2'}, dimensions={0}, use_global_device_ids=true | all-gather | bytes 297216 | tf_op jit(solution)/shard_map/all_gather | solution.py:20
  42.4 10.8 %all-gather = bf16[12,2,336,8]{2,3,1,0:T(8,128)(2,1)S(1)} all-gather(bf16[3,2,336,8]{2,3,1,0:T(8,128)(2,1)S(1)} %split.9), channel_id=2, replica_groups=mesh['cuts_0'=2,'cuts_1'=2,'mode_0'=4,'mode_1'=4,'mode_2'=8] {'mode_0'}, dimensions={0}, use_global_device_ids=true | all-gather | bytes 161280 | tf_op jit(solution)/shard_map/all_gather | solution.py:20
  53.2 29.4 %all_gather.28 = bf16[32,3,2,336,8]{3,4,2,1,0:T(8,128)(2,1)} all-gather(bf16[4,3,2,336,8]{3,4,2,1,0:T(8,128)(2,1)S(1)} %bitcast.161), channel_id=1, replica_groups=mesh['cuts_0'=2,'cuts_1'=2,'mode_0'=4,'mode_1'=4,'mode_2'=8] {'mode_2'}, dimensions={0}, use_global_device_ids=true | all-gather | bytes 1161216 | tf_op jit(solution)/shard_map/all_gather | solution.py:20
  82.6 13.6 %all-gather.1 = bf16[12,2,344,8]{2,3,1,0:T(8,128)(2,1)S(1)} all-gather(bf16[3,2,344,8]{2,3,1,0:T(8,128)(2,1)S(1)} %get-tuple-element.13), channel_id=3, replica_groups=mesh['cuts_0'=2,'cuts_1'=2,'mode_0'=4,'mode_1'=4,'mode_2'=8] {'mode_1'}, dimensions={0}, use_global_device_ids=true | all-gather | bytes 165120 | tf_op jit(solution)/shard_map/all_gather | solution.py:20
  96.3 13.6 %all_gather.31 = bf16[16,3,2,344,8]{3,4,2,1,0:T(8,128)(2,1)} all-gather(bf16[4,3,2,344,8]{3,4,2,1,0:T(8,128)(2,1)S(1)} %bitcast.162), channel_id=1, replica_groups=mesh['cuts_0'=2,'cuts_1'=2,'mode_0'=4,'mode_1'=4,'mode_2'=8] {'mode_0'}, dimensions={0}, use_global_device_ids=true | all-gather | bytes 660480 | tf_op jit(solution)/shard_map/all_gather | solution.py:20
  110.5 1.6 copy.70
  112.9 3.7 gather_fusion.1
  116.6 3.7 broadcast_select_fusion.2
  120.4 0.9 copy.45
  121.3 11.7 %all-to-all-start = ((bf16[2,128,8,128]{3,2,0,1:T(8,128)(2,1)}), bf16[2,128,8,128]{3,2,0,1:T(8,128)(2,1)S(1)}, u32[]{:S(2)}, u32[]{:S(2)}) async-start(bf16[2,128,8,128]{3,2,0,1:T(8,128)(2,1)} %copy.45), calls=%async_computation | async-start | bytes 1048576 | tf_op jit(solution)/shard_map/all_to_all | solution.py:69
  133.0 1.4 fusion.47
  136.4 48.8 %all-gather.8.cloned.1.call-done = bf16[128,3,2,336,8]{3,4,2,1,0:T(8,128)(2,1)} async-done(((bf16[32,3,2,336,8]{3,4,2,1,0:T(8,128)(2,1)}), bf16[128,3,2,336,8]{3,4,2,1,0:T(8,128)(2,1)}) %all-gather.8.cloned.1.call-update) | async-done | bytes 4128784 | tf_op jit(solution)/shard_map/all_gather | solution.py:20
  185.1 5.2 copy.41
  190.4 61.7 %all-gather.10.cloned.1.call-done = bf16[128,3,2,344,8]{3,4,2,1,0:T(8,128)(2,1)} async-done(((bf16[16,3,2,344,8]{3,4,2,1,0:T(8,128)(2,1)}), bf16[128,3,2,344,8]{3,4,2,1,0:T(8,128)(2,1)}) %all-gather.10.cloned.1.call-update) | async-done | bytes 4227088 | tf_op jit(solution)/shard_map/all_gather | solution.py:20
  252.0 5.2 copy.42
  257.2 51.9 %all-gather.14.cloned.1.call-done = bf16[128,3,2,344,8]{3,4,2,1,0:T(8,128)(2,1)} async-done(((bf16[32,3,2,344,8]{3,4,2,1,0:T(8,128)(2,1)}), bf16[128,3,2,344,8]{3,4,2,1,0:T(8,128)(2,1)}) %all-gather.14.cloned.1.call-update) | async-done | bytes 4227088 | tf_op jit(solution)/shard_map/all_gather | solution.py:20
  309.1 13.7 %copy_bitcast_fusion = bf16[3,2,1024,1024]{2,3,1,0:T(8,128)(2,1)} fusion(bf16[128,3,2,344,8]{3,4,2,1,0:T(8,128)(2,1)} %all-gather.14.cloned.1.call-done, bf16[128,3,2,344,8]{3,4,2,1,0:T(8,128)(2,1)} %bitcast.153, bf16[128,3,2,336,8]{3,4,2,1,0:T(8,128)(2,1)} %bitcast.152), kind=kLoop, calls=%fused_computation.5 | loop fusion | flops 37748736 | bytes 25165824 | tf_op jit(solution)/shard_map/reshape | solution.py:30
  322.9 2.3 fusion.5
  325.2 2.3 fusion.4
  327.5 2.3 fusion.28
  329.8 2.3 fusion.29
  332.7 3.7 gather_fusion.2
  336.4 3.7 broadcast_select_fusion.1
  340.2 0.9 copy.49
  341.0 14.8 %all-to-all-start.1 = ((bf16[2,128,8,128]{3,2,0,1:T(8,128)(2,1)}), bf16[2,128,8,128]{3,2,0,1:T(8,128)(2,1)S(1)}, u32[]{:S(2)}, u32[]{:S(2)}) async-start(bf16[2,128,8,128]{3,2,0,1:T(8,128)(2,1)} %copy.49), calls=%async_computation.1 | async-start | bytes 1048576 | tf_op jit(solution)/shard_map/all_to_all | solution.py:69
  357.9 15.8 %all-to-all-done.1 = bf16[2,128,8,128]{3,2,0,1:T(8,128)(2,1)S(1)} async-done(((bf16[2,128,8,128]{3,2,0,1:T(8,128)(2,1)}), bf16[2,128,8,128]{3,2,0,1:T(8,128)(2,1)S(1)}, u32[]{:S(2)}, u32[]{:S(2)}) %all-to-all-start.1) | async-done | bytes 524320 | tf_op jit(solution)/shard_map/all_to_all | solution.py:69
  373.6 2.3 fusion.3
  375.9 2.3 fusion.2
  378.2 2.3 fusion.26
  380.5 2.3 fusion.27
  383.4 3.7 gather_fusion.3
  387.1 3.7 broadcast_select_fusion
  390.9 0.9 copy.53
  391.8 8.2 %all-to-all-start.2 = ((bf16[2,128,8,128]{3,2,0,1:T(8,128)(2,1)}), bf16[2,128,8,128]{3,2,0,1:T(8,128)(2,1)S(1)}, u32[]{:S(2)}, u32[]{:S(2)}) async-start(bf16[2,128,8,128]{3,2,0,1:T(8,128)(2,1)} %copy.53), calls=%async_computation.2 | async-start | bytes 1048576 | tf_op jit(solution)/shard_map/all_to_all | solution.py:69
  401.9 15.7 %all-to-all-done.2 = bf16[2,128,8,128]{3,2,0,1:T(8,128)(2,1)S(1)} async-done(((bf16[2,128,8,128]{3,2,0,1:T(8,128)(2,1)}), bf16[2,128,8,128]{3,2,0,1:T(8,128)(2,1)S(1)}, u32[]{:S(2)}, u32[]{:S(2)}) %all-to-all-start.2) | async-done | bytes 524320 | tf_op jit(solution)/shard_map/all_to_all | solution.py:69
  417.5 2.3 fusion.1
  419.8 2.3 fusion
  422.1 2.3 fusion.24
  424.4 2.3 fusion.25
  428.4 1.2 pad_maximum_fusion.3
  429.6 20.3 %copy.56 = bf16[2,131072]{0,1:T(8,128)(2,1)} copy(bf16[2,131072]{1,0:T(2,128)(2,1)S(1)} %pad_maximum_fusion.3) | data formatting | bytes 1048576 | tf_op jit(solution)/shard_map/stack | solution.py:57
  449.8 21.6 %gather_fusion = bf16[2048,2]{1,0:T(8,128)(2,1)S(1)} fusion(bf16[2,131072]{0,1:T(8,128)(2,1)} %copy.56, s32[2048]{0:T(1024)S(1)} %broadcast_clamp_fusion), kind=kCustom, calls=%fused_computation.3 | custom fusion | bytes 24576 | tf_op jit(solution)/shard_map/jit(_take)/gather | solution.py:79
  472.2 28.2 %psum.35 = f32[2,2048]{0,1:T(8,128)S(1)} all-reduce(f32[2,2048]{0,1:T(8,128)S(1)} %select_bitcast_fusion), channel_id=1, replica_groups=mesh['cuts_0'=2,'cuts_1'=2,'mode_0'=4,'mode_1'=4,'mode_2'=8] {'cuts_0'}, use_global_device_ids=true, to_apply=%region_0.0 | all-reduce | flops 4096 | bytes 32768 | tf_op jit(solution)/shard_map/psum | solution.py:45
  500.5 5.7 psum.36
  506.1 44.0 %psum.37 = f32[2,2048]{0,1:T(8,128)S(1)} all-reduce(f32[2,2048]{0,1:T(8,128)S(1)} %psum.36), channel_id=1, replica_groups=mesh['cuts_0'=2,'cuts_1'=2,'mode_0'=4,'mode_1'=4,'mode_2'=8] {'mode_0'}, use_global_device_ids=true, to_apply=%region_2.4 | all-reduce | flops 4096 | bytes 32768 | tf_op jit(solution)/shard_map/psum | solution.py:45
  550.2 53.7 %psum.38 = f32[2,2048]{0,1:T(8,128)S(1)} all-reduce(f32[2,2048]{0,1:T(8,128)S(1)} %psum.37), channel_id=1, replica_groups=mesh['cuts_0'=2,'cuts_1'=2,'mode_0'=4,'mode_1'=4,'mode_2'=8] {'mode_1'}, use_global_device_ids=true, to_apply=%region_3.5 | all-reduce | flops 4096 | bytes 32768 | tf_op jit(solution)/shard_map/psum | solution.py:45
  603.9 60.6 %psum.39 = f32[2,2048]{0,1:T(8,128)S(1)} all-reduce(f32[2,2048]{0,1:T(8,128)S(1)} %psum.38), channel_id=1, replica_groups=mesh['cuts_0'=2,'cuts_1'=2,'mode_0'=4,'mode_1'=4,'mode_2'=8] {'mode_2'}, use_global_device_ids=true, to_apply=%region_4.6 | all-reduce | flops 4096 | bytes 32768 | tf_op jit(solution)/shard_map/psum | solution.py:45
  (33 shorter events, 6.7 us)
Async XLA Ops:
  7.2 102.8 %all-gather.12.cloned.1.call-start = ((), (), s32[]{:S(2)}) async-start(), calls=%async_computation.5 | async-start | bytes 1474560 | tf_op jit(solution)/shard_map/all_gather | solution.py:20
  41.6 143.6 %all-gather.8.cloned.1.call-start = ((), (), s32[]{:S(2)}) async-start(), calls=%async_computation.3 | async-start | bytes 5898240 | tf_op jit(solution)/shard_map/all_gather | solution.py:20
  82.6 169.5 %all-gather.10.cloned.1.call-start = ((), (), s32[]{:S(2)}) async-start(), calls=%async_computation.4 | async-start | bytes 5308416 | tf_op jit(solution)/shard_map/all_gather | solution.py:20
  109.9 199.2 %all-gather.14.cloned.1.call-start = ((), (), s32[]{:S(2)}) async-start(), calls=%async_computation.6 | async-start | bytes 5898240 | tf_op jit(solution)/shard_map/all_gather | solution.py:20
  121.3 201.6 %all-to-all-start = ((bf16[2,128,8,128]{3,2,0,1:T(8,128)(2,1)}), bf16[2,128,8,128]{3,2,0,1:T(8,128)(2,1)S(1)}, u32[]{:S(2)}, u32[]{:S(2)}) async-start(bf16[2,128,8,128]{3,2,0,1:T(8,128)(2,1)} %copy.45), calls=%async_computation | async-start | bytes 1048576 | tf_op jit(solution)/shard_map/all_to_all | solution.py:69
  332.1 69.7 %copy-start = (s32[2048]{0:T(1024)S(1)}, s32[2048]{0:T(1024)}, u32[]{:S(2)}) copy-start(s32[2048]{0:T(1024)} %param.13) | copy-start | bytes 24580
  332.1 69.7 %copy-start.1 = (s32[2048]{0:T(1024)S(1)}, s32[2048]{0:T(1024)}, u32[]{:S(2)}) copy-start(s32[2048]{0:T(1024)} %param.12) | copy-start | bytes 24580
  341.0 32.6 %all-to-all-start.1 = ((bf16[2,128,8,128]{3,2,0,1:T(8,128)(2,1)}), bf16[2,128,8,128]{3,2,0,1:T(8,128)(2,1)S(1)}, u32[]{:S(2)}, u32[]{:S(2)}) async-start(bf16[2,128,8,128]{3,2,0,1:T(8,128)(2,1)} %copy.49), calls=%async_computation.1 | async-start | bytes 1048576 | tf_op jit(solution)/shard_map/all_to_all | solution.py:69
  391.8 25.8 %all-to-all-start.2 = ((bf16[2,128,8,128]{3,2,0,1:T(8,128)(2,1)}), bf16[2,128,8,128]{3,2,0,1:T(8,128)(2,1)S(1)}, u32[]{:S(2)}, u32[]{:S(2)}) async-start(bf16[2,128,8,128]{3,2,0,1:T(8,128)(2,1)} %copy.53), calls=%async_computation.2 | async-start | bytes 1048576 | tf_op jit(solution)/shard_map/all_to_all | solution.py:69
Sparse Core Ops, SparseCore 0:
  41.7 36.6 all-gather.11
  82.7 102.4 all-gather.7
  187.2 64.7 all-gather.9
  254.0 55.1 all-gather.13
where the time goes:
time: 673 us; the launch traced here: 672 us
  blocking collectives  293 us (44%)
  waiting for transfers between devices  194 us (29%)
  local copies, waits for them, and re-layouts  74.1 us (11%)
  starting transfers between devices  34.8 us (5%)
  other arithmetic  27.9 us (4%)
  matrix products  27.6 us (4%)
  between operations  19.9 us (3%)
    psum x5, blocking collectives, over_axes(): shard = lax.psum(shard, axis)  192 us
    all_gather x4, waiting for transfers between devices, gather_in_order(): blocks = lax.all_gather(blocks, axes[k], axis=0, tiled=True)  162 us
    all_gather x5, blocking collectives, gather_in_order(): blocks = lax.all_gather(blocks, axes[k], axis=0, tiled=True)  101 us
    all_to_all x3, starting transfers between devices, body(): lax.all_to_all(view, MODE, split_axis=1, concat_axis=1, tiled=True)  34.7 us
    all_to_all x3, waiting for transfers between devices, body(): lax.all_to_all(view, MODE, split_axis=1, concat_axis=1, tiled=True)  31.4 us
    dot_general x12, matrix products, product(): lax.dot_general(left, right, numbers, preferred_element_type=jnp.float32)  27.6 us
    another operation x4, local copies, waits for them, and re-layouts, absorb(): return jnp.stack([real, imag], axis=0)  22.1 us
    gather x1, local copies, waits for them, and re-layouts, body(): values = jnp.take(flat, flat_index, axis=1).astype(jnp.float32)  21.6 us
  transfers between devices with their start and end apart: 7, of which 5 were waited for; matrix products, arithmetic and copies ran while one was open for 6% of the time, Pallas kernels for 0%

commit v1 on v0

--- a/solution.py
+++ b/solution.py
@@ -42,7 +42,7 @@
 
 def over_axes(shard, axes):
     for axis in axes:
-        shard = lax.psum(shard, axis)
+        shard = jnp.sum(lax.all_gather(shard, axis), axis=0)
     return shard
 
 

time: 673 us -> 541 us (0.80)
  the two profiles are of different devices: /device:TPU:4 before, /device:TPU:8 now
where the time goes in v1:
time: 541 us; the launch traced here: 540 us
  waiting for transfers between devices  198 us (37%)
  blocking collectives  161 us (30%)
  local copies, waits for them, and re-layouts  75 us (14%)
  starting transfers between devices  30.4 us (6%)
  matrix products  27.6 us (5%)
  other arithmetic  27.3 us (5%)
  between operations  19.9 us (4%)
    all_gather x4, waiting for transfers between devices, gather_in_order(): blocks = lax.all_gather(blocks, axes[k], axis=0, tiled=True)  163 us
    all_gather x5, blocking collectives, gather_in_order(): blocks = lax.all_gather(blocks, axes[k], axis=0, tiled=True)  102 us
    all_gather x5, blocking collectives, over_axes(): shard = jnp.sum(lax.all_gather(shard, axis), axis=0)  58.8 us
    all_to_all x3, waiting for transfers between devices, body(): lax.all_to_all(view, MODE, split_axis=1, concat_axis=1, tiled=True)  34.1 us
    all_to_all x3, starting transfers between devices, body(): lax.all_to_all(view, MODE, split_axis=1, concat_axis=1, tiled=True)  30.2 us
    dot_general x12, matrix products, product(): lax.dot_general(left, right, numbers, preferred_element_type=jnp.float32)  27.6 us
    another operation x4, local copies, waits for them, and re-layouts, absorb(): return jnp.stack([real, imag], axis=0)  22.1 us
    gather x2, local copies, waits for them, and re-layouts, body(): values = jnp.take(flat, flat_index, axis=1).astype(jnp.float32)  21.8 us
  transfers between devices with their start and end apart: 7, of which 5 were waited for; matrix products, arithmetic and copies ran while one was open for 7% of the time, Pallas kernels for 0%

profile of v1, /device:TPU:8, one launch (start us, length us, event | category | flops | bytes accessed | tf_op | source)
XLA Modules:
  0.0 539.5 jit_solution(5348499695694887027)
XLA Ops:
  7.2 0.9 fusion.45
  8.1 33.4 %all-gather.2 = bf16[24,2,344,8]{2,3,1,0:T(8,128)(2,1)} all-gather(bf16[3,2,344,8]{2,3,1,0:T(8,128)(2,1)S(1)} %get-tuple-element.4), channel_id=4, replica_groups=mesh['cuts_0'=2,'cuts_1'=2,'mode_0'=4,'mode_1'=4,'mode_2'=8] {'mode_2'}, dimensions={0}, use_global_device_ids=true | all-gather | bytes 297216 | tf_op jit(solution)/shard_map/all_gather | solution.py:20
  42.4 12.4 %all-gather = bf16[12,2,336,8]{2,3,1,0:T(8,128)(2,1)S(1)} all-gather(bf16[3,2,336,8]{2,3,1,0:T(8,128)(2,1)S(1)} %split.9), channel_id=2, replica_groups=mesh['cuts_0'=2,'cuts_1'=2,'mode_0'=4,'mode_1'=4,'mode_2'=8] {'mode_0'}, dimensions={0}, use_global_device_ids=true | all-gather | bytes 161280 | tf_op jit(solution)/shard_map/all_gather | solution.py:20
  54.7 29.3 %all_gather.56 = bf16[32,3,2,336,8]{3,4,2,1,0:T(8,128)(2,1)} all-gather(bf16[4,3,2,336,8]{3,4,2,1,0:T(8,128)(2,1)S(1)} %bitcast.168), channel_id=1, replica_groups=mesh['cuts_0'=2,'cuts_1'=2,'mode_0'=4,'mode_1'=4,'mode_2'=8] {'mode_2'}, dimensions={0}, use_global_device_ids=true | all-gather | bytes 1161216 | tf_op jit(solution)/shard_map/all_gather | solution.py:20
  84.2 13.6 %all-gather.1 = bf16[12,2,344,8]{2,3,1,0:T(8,128)(2,1)S(1)} all-gather(bf16[3,2,344,8]{2,3,1,0:T(8,128)(2,1)S(1)} %get-tuple-element.3), channel_id=3, replica_groups=mesh['cuts_0'=2,'cuts_1'=2,'mode_0'=4,'mode_1'=4,'mode_2'=8] {'mode_1'}, dimensions={0}, use_global_device_ids=true | all-gather | bytes 165120 | tf_op jit(solution)/shard_map/all_gather | solution.py:20
  97.8 13.6 %all_gather.59 = bf16[16,3,2,344,8]{3,4,2,1,0:T(8,128)(2,1)} all-gather(bf16[4,3,2,344,8]{3,4,2,1,0:T(8,128)(2,1)S(1)} %bitcast.169), channel_id=1, replica_groups=mesh['cuts_0'=2,'cuts_1'=2,'mode_0'=4,'mode_1'=4,'mode_2'=8] {'mode_0'}, dimensions={0}, use_global_device_ids=true | all-gather | bytes 660480 | tf_op jit(solution)/shard_map/all_gather | solution.py:20
  112.0 1.6 copy.90
  114.5 3.7 gather_fusion.1
  118.2 3.7 broadcast_select_fusion.2
  121.9 0.9 copy.62
  122.8 9.8 %all-to-all-start = ((bf16[2,128,8,128]{3,2,0,1:T(8,128)(2,1)}), bf16[2,128,8,128]{3,2,0,1:T(8,128)(2,1)S(1)}, u32[]{:S(2)}, u32[]{:S(2)}) async-start(bf16[2,128,8,128]{3,2,0,1:T(8,128)(2,1)} %copy.62), calls=%async_computation | async-start | bytes 1048576 | tf_op jit(solution)/shard_map/all_to_all | solution.py:69
  132.6 1.4 fusion.47
  136.0 51.9 %all-gather.16.cloned.1.call-done = bf16[128,3,2,336,8]{3,4,2,1,0:T(8,128)(2,1)} async-done(((bf16[32,3,2,336,8]{3,4,2,1,0:T(8,128)(2,1)}), bf16[128,3,2,336,8]{3,4,2,1,0:T(8,128)(2,1)}) %all-gather.16.cloned.1.call-update) | async-done | bytes 4128784 | tf_op jit(solution)/shard_map/all_gather | solution.py:20
  187.9 5.2 copy.58
  193.1 58.9 %all-gather.18.cloned.1.call-done = bf16[128,3,2,344,8]{3,4,2,1,0:T(8,128)(2,1)} async-done(((bf16[16,3,2,344,8]{3,4,2,1,0:T(8,128)(2,1)}), bf16[128,3,2,344,8]{3,4,2,1,0:T(8,128)(2,1)}) %all-gather.18.cloned.1.call-update) | async-done | bytes 4227088 | tf_op jit(solution)/shard_map/all_gather | solution.py:20
  252.0 5.2 copy.59
  257.2 52.7 %all-gather.22.cloned.1.call-done = bf16[128,3,2,344,8]{3,4,2,1,0:T(8,128)(2,1)} async-done(((bf16[32,3,2,344,8]{3,4,2,1,0:T(8,128)(2,1)}), bf16[128,3,2,344,8]{3,4,2,1,0:T(8,128)(2,1)}) %all-gather.22.cloned.1.call-update) | async-done | bytes 4227088 | tf_op jit(solution)/shard_map/all_gather | solution.py:20
  309.9 13.7 %copy_bitcast_fusion = bf16[3,2,1024,1024]{2,3,1,0:T(8,128)(2,1)} fusion(bf16[128,3,2,344,8]{3,4,2,1,0:T(8,128)(2,1)} %all-gather.22.cloned.1.call-done, bf16[128,3,2,344,8]{3,4,2,1,0:T(8,128)(2,1)} %bitcast.159, bf16[128,3,2,336,8]{3,4,2,1,0:T(8,128)(2,1)} %bitcast.158), kind=kLoop, calls=%fused_computation.5 | loop fusion | flops 37748736 | bytes 25165824 | tf_op jit(solution)/shard_map/reshape | solution.py:30
  323.7 2.3 fusion.5
  326.0 2.3 fusion.4
  328.3 2.3 fusion.28
  330.6 2.3 fusion.29
  333.5 3.7 gather_fusion.2
  337.2 3.7 broadcast_select_fusion.1
  341.0 0.9 copy.66
  341.8 13.6 %all-to-all-start.1 = ((bf16[2,128,8,128]{3,2,0,1:T(8,128)(2,1)}), bf16[2,128,8,128]{3,2,0,1:T(8,128)(2,1)S(1)}, u32[]{:S(2)}, u32[]{:S(2)}) async-start(bf16[2,128,8,128]{3,2,0,1:T(8,128)(2,1)} %copy.66), calls=%async_computation.1 | async-start | bytes 1048576 | tf_op jit(solution)/shard_map/all_to_all | solution.py:69
  357.5 17.1 %all-to-all-done.1 = bf16[2,128,8,128]{3,2,0,1:T(8,128)(2,1)S(1)} async-done(((bf16[2,128,8,128]{3,2,0,1:T(8,128)(2,1)}), bf16[2,128,8,128]{3,2,0,1:T(8,128)(2,1)S(1)}, u32[]{:S(2)}, u32[]{:S(2)}) %all-to-all-start.1) | async-done | bytes 524320 | tf_op jit(solution)/shard_map/all_to_all | solution.py:69
  374.6 2.3 fusion.3
  376.9 2.3 fusion.2
  379.2 2.3 fusion.26
  381.5 2.3 fusion.27
  384.4 3.7 gather_fusion.3
  388.1 3.7 broadcast_select_fusion
  391.9 0.9 copy.70
  392.7 6.8 %all-to-all-start.2 = ((bf16[2,128,8,128]{3,2,0,1:T(8,128)(2,1)}), bf16[2,128,8,128]{3,2,0,1:T(8,128)(2,1)S(1)}, u32[]{:S(2)}, u32[]{:S(2)}) async-start(bf16[2,128,8,128]{3,2,0,1:T(8,128)(2,1)} %copy.70), calls=%async_computation.2 | async-start | bytes 1048576 | tf_op jit(solution)/shard_map/all_to_all | solution.py:69
  401.5 17.0 %all-to-all-done.2 = bf16[2,128,8,128]{3,2,0,1:T(8,128)(2,1)S(1)} async-done(((bf16[2,128,8,128]{3,2,0,1:T(8,128)(2,1)}), bf16[2,128,8,128]{3,2,0,1:T(8,128)(2,1)S(1)}, u32[]{:S(2)}, u32[]{:S(2)}) %all-to-all-start.2) | async-done | bytes 524320 | tf_op jit(solution)/shard_map/all_to_all | solution.py:69
  418.5 2.3 fusion.1
  420.8 2.3 fusion
  423.1 2.3 fusion.24
  425.4 2.3 fusion.25
  429.4 1.2 pad_maximum_fusion.3
  430.6 20.3 %copy.73 = bf16[2,131072]{0,1:T(8,128)(2,1)} copy(bf16[2,131072]{1,0:T(2,128)(2,1)S(1)} %pad_maximum_fusion.3) | data formatting | bytes 1048576 | tf_op jit(solution)/shard_map/stack | solution.py:57
  450.8 21.6 %gather_fusion = bf16[2048,2]{1,0:T(8,128)(2,1)S(1)} fusion(bf16[2,131072]{0,1:T(8,128)(2,1)} %copy.73, s32[2048]{0:T(1024)S(1)} %broadcast_clamp_fusion), kind=kCustom, calls=%fused_computation.3 | custom fusion | bytes 24576 | tf_op jit(solution)/shard_map/jit(_take)/gather | solution.py:79
  472.7 8.3 %all_gather.64 = f32[2,2,2048]{2,1,0:T(2,128)S(1)} all-gather(f32[1,2,2048]{2,1,0:T(2,128)S(1)} %convert_select_fusion), channel_id=1, replica_groups=mesh['cuts_0'=2,'cuts_1'=2,'mode_0'=4,'mode_1'=4,'mode_2'=8] {'cuts_0'}, dimensions={0}, use_global_device_ids=true | all-gather | bytes 49152 | tf_op jit(solution)/shard_map/all_gather | solution.py:45
  481.7 1.8 all-gather.7
  483.6 11.9 %all-gather.8 = f32[4,2,2048]{2,1,0:T(2,128)S(1)} all-gather(f32[1,2,2048]{2,1,0:T(2,128)S(1)} %bitcast.170), channel_id=6, replica_groups=mesh['cuts_0'=2,'cuts_1'=2,'mode_0'=4,'mode_1'=4,'mode_2'=8] {'mode_0'}, dimensions={0}, use_global_device_ids=true | all-gather | bytes 81920 | tf_op jit(solution)/shard_map/all_gather | solution.py:45
  495.5 12.2 %all-gather.9 = f32[4,2,2048]{2,1,0:T(2,128)S(1)} all-gather(f32[1,2,2048]{2,1,0:T(2,128)S(1)} %bitcast.171), channel_id=7, replica_groups=mesh['cuts_0'=2,'cuts_1'=2,'mode_0'=4,'mode_1'=4,'mode_2'=8] {'mode_1'}, dimensions={0}, use_global_device_ids=true | all-gather | bytes 81920 | tf_op jit(solution)/shard_map/all_gather | solution.py:45
  507.7 24.6 %all-gather.10 = f32[8,2,2048]{2,1,0:T(2,128)S(1)} all-gather(f32[1,2,2048]{2,1,0:T(2,128)S(1)} %bitcast.172), channel_id=8, replica_groups=mesh['cuts_0'=2,'cuts_1'=2,'mode_0'=4,'mode_1'=4,'mode_2'=8] {'mode_2'}, dimensions={0}, use_global_device_ids=true | all-gather | bytes 147456 | tf_op jit(solution)/shard_map/all_gather | solution.py:45
  (40 shorter events, 7.0 us)
Async XLA Ops:
  7.2 104.4 %all-gather.20.cloned.1.call-start = ((), (), s32[]{:S(2)}) async-start(), calls=%async_computation.5 | async-start | bytes 1474560 | tf_op jit(solution)/shard_map/all_gather | solution.py:20
  41.6 146.4 %all-gather.16.cloned.1.call-start = ((), (), s32[]{:S(2)}) async-start(), calls=%async_computation.3 | async-start | bytes 5898240 | tf_op jit(solution)/shard_map/all_gather | solution.py:20
  84.1 167.9 %all-gather.18.cloned.1.call-start = ((), (), s32[]{:S(2)}) async-start(), calls=%async_computation.4 | async-start | bytes 5308416 | tf_op jit(solution)/shard_map/all_gather | solution.py:20
  111.4 198.5 %all-gather.22.cloned.1.call-start = ((), (), s32[]{:S(2)}) async-start(), calls=%async_computation.6 | async-start | bytes 5898240 | tf_op jit(solution)/shard_map/all_gather | solution.py:20
  122.8 200.9 %all-to-all-start = ((bf16[2,128,8,128]{3,2,0,1:T(8,128)(2,1)}), bf16[2,128,8,128]{3,2,0,1:T(8,128)(2,1)S(1)}, u32[]{:S(2)}, u32[]{:S(2)}) async-start(bf16[2,128,8,128]{3,2,0,1:T(8,128)(2,1)} %copy.62), calls=%async_computation | async-start | bytes 1048576 | tf_op jit(solution)/shard_map/all_to_all | solution.py:69
  332.9 68.6 %copy-start = (s32[2048]{0:T(1024)S(1)}, s32[2048]{0:T(1024)}, u32[]{:S(2)}) copy-start(s32[2048]{0:T(1024)} %param.13) | copy-start | bytes 24580
  332.9 68.6 %copy-start.1 = (s32[2048]{0:T(1024)S(1)}, s32[2048]{0:T(1024)}, u32[]{:S(2)}) copy-start(s32[2048]{0:T(1024)} %param.12) | copy-start | bytes 24580
  341.8 32.8 %all-to-all-start.1 = ((bf16[2,128,8,128]{3,2,0,1:T(8,128)(2,1)}), bf16[2,128,8,128]{3,2,0,1:T(8,128)(2,1)S(1)}, u32[]{:S(2)}, u32[]{:S(2)}) async-start(bf16[2,128,8,128]{3,2,0,1:T(8,128)(2,1)} %copy.66), calls=%async_computation.1 | async-start | bytes 1048576 | tf_op jit(solution)/shard_map/all_to_all | solution.py:69
  392.7 25.8 %all-to-all-start.2 = ((bf16[2,128,8,128]{3,2,0,1:T(8,128)(2,1)}), bf16[2,128,8,128]{3,2,0,1:T(8,128)(2,1)S(1)}, u32[]{:S(2)}, u32[]{:S(2)}) async-start(bf16[2,128,8,128]{3,2,0,1:T(8,128)(2,1)} %copy.70), calls=%async_computation.2 | async-start | bytes 1048576 | tf_op jit(solution)/shard_map/all_to_all | solution.py:69
Sparse Core Ops, SparseCore 0:
  41.7 35.2 all-gather.19
  84.2 103.6 all-gather.15
  190.0 61.9 all-gather.17
  253.9 55.9 all-gather.21
